TPU v7x, 128 devices: a whole 4x4x4 slice. The times are simulated.
128 devices in a mesh: vocab: 8 (over x_lo, y), dp: 8 (over z, core), teacher: 2 (over x_hi).
Axes of the slice: x: 4 (x_hi: 2, x_lo: 2; x = x_hi * 2 + x_lo), y: 4, z: 4, core: 2. Of those that a mesh axis runs over, the one named last changes fastest.
Arguments:
- hidden_states: bfloat16 [2048, 4096], P('teacher'), may hold values from -300 to 300
- head_weight: bfloat16 [4096, 65536], P(None, ('vocab', 'dp')), may hold values from -3 to 3
- teacher_logits: bfloat16 [2048, 65536], P(None, ('vocab', 'dp', 'teacher')), may hold values from -20 to 460
- token_weight: float32 [2048], P('teacher'), may hold values from 2 to 20
Outputs:
- hidden_grad: bfloat16 [2048, 4096], P('teacher', ('vocab', 'dp'))
- weight_grad: bfloat16 [4096, 65536], P('teacher', ('vocab', 'dp'))
All inputs are finite; a program needn't handle non-finite values.
Results may differ from a plain program's by a relative error of at most 0.005.
Values may be sent and summed in bfloat16 or wider, within the bound.
No kernel may reach another device: no remote copies, remote signals or barrier semaphores. Data moves between devices by JAX's collectives and lax.ppermute only.
A program may use at most 192 MiB of HBM per device.

v0:
```python
import jax
import jax.numpy as jnp
from jax import lax
from jax.sharding import PartitionSpec as P


def per_device(hidden_states, head_weight, teacher_logits, token_weight):
    teacher = lax.all_to_all(
        teacher_logits, "teacher", split_axis=0, concat_axis=1, tiled=True
    ).astype(jnp.float32)
    logits = jnp.dot(hidden_states, head_weight, preferred_element_type=jnp.float32)
    student_top = jnp.max(logits, axis=1)
    teacher_top = jnp.max(teacher, axis=1)
    student_top, teacher_top = lax.pmax((student_top, teacher_top), ("vocab", "dp"))
    student_total = jnp.sum(jnp.exp(logits - student_top[:, None]), axis=1)
    teacher_total = jnp.sum(jnp.exp(teacher - teacher_top[:, None]), axis=1)
    student_total, teacher_total = lax.psum((student_total, teacher_total), ("vocab", "dp"))
    student_norm = student_top + jnp.log(student_total)
    teacher_norm = teacher_top + jnp.log(teacher_total)
    logit_grad = (
        token_weight[:, None]
        * (jnp.exp(logits - student_norm[:, None]) - jnp.exp(teacher - teacher_norm[:, None]))
    ).astype(jnp.bfloat16)
    hidden_share = lax.psum_scatter(
        lax.dot_general(
            head_weight, logit_grad, (((1,), (1,)), ((), ())), preferred_element_type=jnp.float32
        ),
        ("vocab", "dp"),
        scatter_dimension=0,
        tiled=True,
    )
    hidden_grad = hidden_share.T.astype(jnp.bfloat16)
    weight_share = lax.psum_scatter(
        lax.dot_general(
            hidden_states, logit_grad, (((0,), (0,)), ((), ())), preferred_element_type=jnp.float32
        ),
        "teacher",
        scatter_dimension=0,
        tiled=True,
    )
    return (hidden_grad, weight_share.astype(jnp.bfloat16))


def solution(mesh):
    return jax.shard_map(
        per_device,
        mesh=mesh,
        in_specs=(
            P("teacher", None),
            P(None, ("vocab", "dp")),
            P(None, ("vocab", "dp", "teacher")),
            P("teacher"),
        ),
        out_specs=(P("teacher", ("vocab", "dp")), P("teacher", ("vocab", "dp"))),
        check_vma=False,
    )
```

profile of v0, /device:TPU:1, one launch (start us, length us, event | category | flops | bytes accessed | tf_op | source)
XLA Modules:
  0.0 890.2 jit_solution(3435739700118504908)
XLA Ops:
  7.2 4.0 copy.9
  11.1 4.8 all-to-all-start
  16.0 0.0 reduce-scatter.7.cloned.1.call-start
  16.0 15.1 %fusion.4 = (f32[1024]{0:T(1024)S(1)}, f32[1024,1024]{0,1:T(8,128)}) fusion(bf16[1024,4096]{1,0:T(8,128)(2,1)} %param.4, bf16[4096,1024]{1,0:T(8,128)(2,1)} %param.5), kind=kOutput, calls=%fused_computation.12 | convolution fusion | flops 8590982144 | bytes 20975616 | tf_op jit(solution)/shard_map/dot_general | solution.py:11
  31.1 0.0 copy-start.2
  31.1 10.4 %all-to-all-done = bf16[2,1024,512]{1,2,0:T(8,128)(2,1)S(1)} async-done(((bf16[2,1024,512]{1,2,0:T(8,128)(2,1)}), bf16[2,1024,512]{1,2,0:T(8,128)(2,1)S(1)}, u32[]{:S(2)}, u32[]{:S(2)}) %all-to-all-start) | async-done | bytes 2097184 | tf_op jit(solution)/shard_map/all_to_all | solution.py:8
  41.4 0.4 reduce_max.24
  41.8 142.9 %all-reduce.1 = (f32[1024]{0:T(1024)S(1)}, f32[1024]{0:T(1024)S(1)}) all-reduce(bf16[1024]{0:T(1024)(128)(2,1)S(1)} %reduce_max.24, f32[1024]{0:T(1024)S(1)} %get-tuple-element.10), channel_id=1, replica_groups=mesh['vocab'=8,'dp'=8,'teacher'=2] {'vocab','dp'}, use_global_device_ids=true, to_apply=%region_5.0 | all-reduce | flops 2048 | bytes 14336 | tf_op jit(solution)/shard_map/pmax | solution.py:14
  184.7 2.8 exponential_reduce_fusion.1
  187.6 0.7 exponential_reduce_fusion
  188.3 145.1 %all-reduce = (f32[1024]{0:T(1024)S(1)}, f32[1024]{0:T(1024)S(1)}) all-reduce(f32[1024]{0:T(1024)S(1)} %exponential_reduce_fusion, f32[1024]{0:T(1024)S(1)} %exponential_reduce_fusion.1), channel_id=1, replica_groups=mesh['vocab'=8,'dp'=8,'teacher'=2] {'vocab','dp'}, use_global_device_ids=true, to_apply=%region_7.0 | all-reduce | flops 2048 | bytes 16384 | tf_op jit(solution)/shard_map/psum | solution.py:17
  333.4 0.0 copy-done.2
  333.4 3.5 fusion.3
  336.9 0.0 copy-start
  336.9 1.3 copy-done
  338.2 14.5 %convolution_bitcast_fusion.1 = f32[4096,1024]{0,1:T(8,128)} fusion(bf16[1024,1024]{0,1:T(8,128)(2,1)S(1)} %fusion.3, bf16[4096,1024]{1,0:T(8,128)(2,1)} %param.5), kind=kOutput, calls=%fused_computation.1 | convolution fusion | flops 8589934592 | bytes 27262976 | tf_op jit(solution)/shard_map/dot_general | solution.py:25
  352.7 17.5 %copy.12 = f32[4096,1024]{1,0:T(8,128)} copy(f32[4096,1024]{0,1:T(8,128)} %convolution_bitcast_fusion.1) | data formatting | bytes 33554432
  370.2 0.0 copy-start.1
  370.2 0.0 reduce-scatter.7.cloned.1.call-update
  370.2 0.0 reduce-scatter.5.cloned.1.call-start
  370.2 1.5 copy-done.1
  371.8 14.5 %convolution_bitcast_fusion = f32[4096,1024]{0,1:T(8,128)} fusion(bf16[1024,1024]{0,1:T(8,128)(2,1)S(1)} %copy-done.1, bf16[1024,4096]{1,0:T(8,128)(2,1)} %param.4), kind=kOutput, calls=%fused_computation | convolution fusion | flops 8589934592 | bytes 27262976 | tf_op jit(solution)/shard_map/dot_general | solution.py:34
  386.3 0.0 reduce-scatter.5.cloned.1.call-update
  386.3 287.1 %reduce-scatter.7.cloned.1.call-done = f32[64,1024]{1,0:T(8,128)} async-done(((f32[4096,1024]{1,0:T(8,128)}), f32[64,1024]{1,0:T(8,128)}) %reduce-scatter.7.cloned.1.call-update) | async-done | bytes 262160
  673.4 1.1 copy.13
  674.6 0.8 copy.10
  675.3 195.6 %reduce-scatter.5.cloned.1.call-done = f32[2048,1024]{0,1:T(8,128)} async-done(((f32[4096,1024]{0,1:T(8,128)}), f32[2048,1024]{0,1:T(8,128)}) %reduce-scatter.5.cloned.1.call-update) | async-done | bytes 8388624 | tf_op jit(solution)/shard_map/reduce_scatter | solution.py:33
  871.0 6.0 convert_element_type.32
  876.9 6.4 copy.11
  (1 shorter events, 0.0 us)
Async XLA Ops:
  11.1 30.3 %all-to-all-start = ((bf16[2,1024,512]{1,2,0:T(8,128)(2,1)}), bf16[2,1024,512]{1,2,0:T(8,128)(2,1)S(1)}, u32[]{:S(2)}, u32[]{:S(2)}) async-start(bf16[2,1024,512]{1,2,0:T(8,128)(2,1)} %copy.9), calls=%async_computation | async-start | bytes 4194304 | tf_op jit(solution)/shard_map/all_to_all | solution.py:8
  16.0 657.5 %reduce-scatter.7.cloned.1.call-start = ((), (), s32[]{:S(2)}) async-start(), calls=%async_computation.4 | async-start | bytes 17039360
  31.1 302.3 %copy-start.2 = (f32[1024]{0:T(1024)S(1)}, f32[1024]{0:T(1024)}, u32[]{:S(2)}) copy-start(f32[1024]{0:T(1024)} %param.7) | copy-start | bytes 12292
  336.9 1.3 copy-start
  370.2 1.6 copy-start.1
  370.2 500.8 %reduce-scatter.5.cloned.1.call-start = ((), (), s32[]{:S(2)}) async-start(), calls=%async_computation.3 | async-start | bytes 25165824 | tf_op jit(solution)/shard_map/reduce_scatter | solution.py:33
Sparse Core Ops, SparseCore 0:
  370.3 303.0 reduce-scatter.6
  675.8 195.0 reduce-scatter.4
where the time goes:
time: 891 us; the launch traced here: 890 us
  waiting for transfers between devices  493 us (55%)
  blocking collectives  288 us (32%)
  matrix products  44.1 us (5%)
  local copies, waits for them, and re-layouts  32.6 us (4%)
  between operations  14.1 us (2%)
  other arithmetic  13.4 us (2%)
    unnamed x3, waiting for transfers between devices  287 us
    reduce_scatter x1, waiting for transfers between devices, per_device(): lax.psum_scatter(lax.dot_general(hidden_states, logit_grad, (((0,), (0,))...  196 us
    psum x1, blocking collectives, per_device(): lax.psum((student_total, teacher_total), ('vocab', 'dp'))  145 us
    pmax x1, blocking collectives, per_device(): lax.pmax((student_top, teacher_top), ('vocab', 'dp'))  143 us
    unnamed x10, local copies, waits for them, and re-layouts  28.6 us
  transfers between devices with their start and end apart: 3, of which 3 were waited for; matrix products, arithmetic and copies ran while one was open for 4% of the time, Pallas kernels for 0%

commit v1 on v0

--- a/solution.py
+++ b/solution.py
@@ -14,7 +14,7 @@
     student_top, teacher_top = lax.pmax((student_top, teacher_top), ("vocab", "dp"))
     student_total = jnp.sum(jnp.exp(logits - student_top[:, None]), axis=1)
     teacher_total = jnp.sum(jnp.exp(teacher - teacher_top[:, None]), axis=1)
-    student_total, teacher_total = lax.psum((student_total, teacher_total), ("vocab", "dp"))
+    student_total, teacher_total = lax.psum(lax.psum((student_total, teacher_total), "vocab"), "dp")
     student_norm = student_top + jnp.log(student_total)
     teacher_norm = teacher_top + jnp.log(teacher_total)
     logit_grad = (

time: 891 us -> 781 us (0.88)
  blocking collectives: 288 us -> 176 us
    psum x1 -> x2, blocking collectives: 145 us -> 33.5 us  [the longest x1 20.7 us: per_device(): lax.psum(lax.psum((student_total, teacher_total), 'vocab'), 'dp')]
where the time goes in v1:
time: 781 us; the launch traced here: 780 us
  waiting for transfers between devices  495 us (63%)
  blocking collectives  176 us (23%)
  matrix products  44 us (6%)
  local copies, waits for them, and re-layouts  32.6 us (4%)
  between operations  14.1 us (2%)
  other arithmetic  13.4 us (2%)
    unnamed x3, waiting for transfers between devices  288 us
    reduce_scatter x1, waiting for transfers between devices, per_device(): lax.psum_scatter(lax.dot_general(hidden_states, logit_grad, (((0,), (0,))...  196 us
    pmax x1, blocking collectives, per_device(): lax.pmax((student_top, teacher_top), ('vocab', 'dp'))  143 us
    unnamed x10, local copies, waits for them, and re-layouts  28.6 us
    psum x1, blocking collectives, per_device(): lax.psum(lax.psum((student_total, teacher_total), 'vocab'), 'dp')  20.7 us
  transfers between devices with their start and end apart: 3, of which 3 were waited for; matrix products, arithmetic and copies ran while one was open for 4% of the time, Pallas kernels for 0%

profile of v1, /device:TPU:1, one launch (start us, length us, event | category | flops | bytes accessed | tf_op | source)
XLA Modules:
  0.0 780.0 jit_solution(1549581924462197513)
XLA Ops:
  7.2 4.0 copy.9
  11.1 4.8 all-to-all-start
  16.0 0.0 reduce-scatter.7.cloned.1.call-start
  16.0 15.1 %fusion.4 = (f32[1024]{0:T(1024)S(1)}, f32[1024,1024]{0,1:T(8,128)}) fusion(bf16[1024,4096]{1,0:T(8,128)(2,1)} %param.4, bf16[4096,1024]{1,0:T(8,128)(2,1)} %param.5), kind=kOutput, calls=%fused_computation.12 | convolution fusion | flops 8590982144 | bytes 20975616 | tf_op jit(solution)/shard_map/dot_general | solution.py:11
  31.1 0.0 copy-start.2
  31.1 10.4 %all-to-all-done = bf16[2,1024,512]{1,2,0:T(8,128)(2,1)S(1)} async-done(((bf16[2,1024,512]{1,2,0:T(8,128)(2,1)}), bf16[2,1024,512]{1,2,0:T(8,128)(2,1)S(1)}, u32[]{:S(2)}, u32[]{:S(2)}) %all-to-all-start) | async-done | bytes 2097184 | tf_op jit(solution)/shard_map/all_to_all | solution.py:8
  41.4 0.4 reduce_max.24
  41.8 142.9 %all-reduce = (f32[1024]{0:T(1024)S(1)}, f32[1024]{0:T(1024)S(1)}) all-reduce(bf16[1024]{0:T(1024)(128)(2,1)S(1)} %reduce_max.24, f32[1024]{0:T(1024)S(1)} %get-tuple-element.12), channel_id=1, replica_groups=mesh['vocab'=8,'dp'=8,'teacher'=2] {'vocab','dp'}, use_global_device_ids=true, to_apply=%region_6.0 | all-reduce | flops 2048 | bytes 14336 | tf_op jit(solution)/shard_map/pmax | solution.py:14
  184.7 2.8 exponential_reduce_fusion.1
  187.6 0.7 exponential_reduce_fusion
  188.3 12.7 %all-reduce.2 = (f32[1024]{0:T(1024)S(1)}, f32[1024]{0:T(1024)S(1)}) all-reduce(f32[1024]{0:T(1024)S(1)} %exponential_reduce_fusion, f32[1024]{0:T(1024)S(1)} %exponential_reduce_fusion.1), channel_id=1, replica_groups=mesh['vocab'=8,'dp'=8,'teacher'=2] {'vocab'}, use_global_device_ids=true, to_apply=%region_8.0 | all-reduce | flops 2048 | bytes 16384 | tf_op jit(solution)/shard_map/psum | solution.py:17
  201.0 20.7 %all-reduce.1 = (f32[1024]{0:T(1024)S(1)}, f32[1024]{0:T(1024)S(1)}) all-reduce(f32[1024]{0:T(1024)S(1)} %get-tuple-element.10, f32[1024]{0:T(1024)S(1)} %get-tuple-element.11), channel_id=1, replica_groups=mesh['vocab'=8,'dp'=8,'teacher'=2] {'dp'}, use_global_device_ids=true, to_apply=%region_9.0 | all-reduce | flops 2048 | bytes 16384 | tf_op jit(solution)/shard_map/psum | solution.py:17
  221.8 0.0 copy-done.2
  221.8 3.5 fusion.3
  225.3 0.0 copy-start
  225.3 1.3 copy-done
  226.6 14.5 %convolution_bitcast_fusion.1 = f32[4096,1024]{0,1:T(8,128)} fusion(bf16[1024,1024]{0,1:T(8,128)(2,1)S(1)} %fusion.3, bf16[4096,1024]{1,0:T(8,128)(2,1)} %param.5), kind=kOutput, calls=%fused_computation.1 | convolution fusion | flops 8589934592 | bytes 27262976 | tf_op jit(solution)/shard_map/dot_general | solution.py:25
  241.1 17.5 %copy.12 = f32[4096,1024]{1,0:T(8,128)} copy(f32[4096,1024]{0,1:T(8,128)} %convolution_bitcast_fusion.1) | data formatting | bytes 33554432
  258.6 0.0 copy-start.1
  258.6 0.0 reduce-scatter.7.cloned.1.call-update
  258.6 0.0 reduce-scatter.5.cloned.1.call-start
  258.6 1.5 copy-done.1
  260.2 14.4 %convolution_bitcast_fusion = f32[4096,1024]{0,1:T(8,128)} fusion(bf16[1024,1024]{0,1:T(8,128)(2,1)S(1)} %copy-done.1, bf16[1024,4096]{1,0:T(8,128)(2,1)} %param.4), kind=kOutput, calls=%fused_computation | convolution fusion | flops 8589934592 | bytes 27262976 | tf_op jit(solution)/shard_map/dot_general | solution.py:34
  274.5 0.0 reduce-scatter.5.cloned.1.call-update
  274.6 287.9 %reduce-scatter.7.cloned.1.call-done = f32[64,1024]{1,0:T(8,128)} async-done(((f32[4096,1024]{1,0:T(8,128)}), f32[64,1024]{1,0:T(8,128)}) %reduce-scatter.7.cloned.1.call-update) | async-done | bytes 262160
  562.4 1.1 copy.13
  563.5 0.8 copy.10
  564.3 196.5 %reduce-scatter.5.cloned.1.call-done = f32[2048,1024]{0,1:T(8,128)} async-done(((f32[4096,1024]{0,1:T(8,128)}), f32[2048,1024]{0,1:T(8,128)}) %reduce-scatter.5.cloned.1.call-update) | async-done | bytes 8388624 | tf_op jit(solution)/shard_map/reduce_scatter | solution.py:33
  760.8 6.0 convert_element_type.32
  766.8 6.4 copy.11
  (1 shorter events, 0.0 us)
Async XLA Ops:
  11.1 30.3 %all-to-all-start = ((bf16[2,1024,512]{1,2,0:T(8,128)(2,1)}), bf16[2,1024,512]{1,2,0:T(8,128)(2,1)S(1)}, u32[]{:S(2)}, u32[]{:S(2)}) async-start(bf16[2,1024,512]{1,2,0:T(8,128)(2,1)} %copy.9), calls=%async_computation | async-start | bytes 4194304 | tf_op jit(solution)/shard_map/all_to_all | solution.py:8
  16.0 546.5 %reduce-scatter.7.cloned.1.call-start = ((), (), s32[]{:S(2)}) async-start(), calls=%async_computation.4 | async-start | bytes 17039360
  31.1 190.7 %copy-start.2 = (f32[1024]{0:T(1024)S(1)}, f32[1024]{0:T(1024)}, u32[]{:S(2)}) copy-start(f32[1024]{0:T(1024)} %param.7) | copy-start | bytes 12292
  225.3 1.3 copy-start
  258.6 1.6 copy-start.1
  258.6 502.2 %reduce-scatter.5.cloned.1.call-start = ((), (), s32[]{:S(2)}) async-start(), calls=%async_computation.3 | async-start | bytes 25165824 | tf_op jit(solution)/shard_map/reduce_scatter | solution.py:33
Sparse Core Ops, SparseCore 0:
  258.7 303.6 reduce-scatter.6
  564.8 195.9 reduce-scatter.4
